TPU v7x, 256 devices: a whole 4x4x8 slice. The times are simulated.
256 devices in a mesh: pairs: 64 (over z, x, core), win: 4 (over y).
Axes of the slice: x: 4, y: 4, z: 8, core: 2. Of those that a mesh axis runs over, the one named last changes fastest.
Arguments:
- raw_traces: bfloat16 [4, 320, 128, 512], P('win', None, 'pairs'), may hold values from -6 to 6
- tile_pairs: int32 [64, 4, 2], replicated, may hold values from -1 to 319, as said below
- block_slot: int32 [320], replicated, may hold values from 0 to 319, as said below
- win_offset: int32 [4], P('win'), may hold values from 0 to 128
Outputs:
- stacks: float32 [128, 256, 128, 128], P('win', 'pairs')
Inputs may be any that keep to these rules, and one draw needn't show every extreme that they name: `tile_pairs`: row p lists owner p's tiles: pairs of block numbers, then rows of -1. Each owner has 1 to 4 tiles and some owner exactly 4. The blocks named in one owner's row are all different. `block_slot`: each slot holds exactly one block.
All inputs are finite; a program needn't handle non-finite values.
Results may differ from a plain program's by a relative error of at most 0.0041.
Values may be sent and summed in bfloat16 or wider, within the bound.
A program may use at most 192 MiB of HBM per device.

v0:
```python
import math
import jax
import jax.numpy as jnp
from jax import lax
from jax.sharding import PartitionSpec as P

LAGS = 128
eps = 1e-06


def whiten(signal):
    length = signal.shape[-1]
    width = LAGS
    radius = LAGS // 2
    seg_count = length // width
    magnitude = jnp.abs(signal).reshape(signal.shape[:-1] + (seg_count, width))
    padded = jnp.pad(magnitude, [(0, 0)] * (magnitude.ndim - 2) + [(1, 1), (0, 0)])
    windows = jnp.concatenate([padded[..., :-2, :], padded[..., 1:-1, :], padded[..., 2:, :]], -1)
    rowpos = jnp.arange(3 * width)[:, None]
    colpos = jnp.arange(width)[None, :]
    band_matrix = (jnp.abs(rowpos - width - colpos) <= radius).astype(jnp.float32)
    totals = jnp.einsum(
        "...ni,ij->...nj", windows, band_matrix, precision=lax.Precision.HIGHEST
    ).reshape(signal.shape)
    position = jnp.arange(length)
    tally = (jnp.minimum(position, radius) + jnp.minimum(length - 1 - position, radius) + 1).astype(
        jnp.float32
    )
    return (signal / (totals / tally + eps)).astype(jnp.bfloat16)


def correlate(leading_blocks, trailing_blocks):
    seg_len = leading_blocks.shape[-1]
    samples = seg_len - LAGS
    half = LAGS // 2
    kernel = jnp.transpose(leading_blocks[..., half : half + samples], (1, 0, 2))
    source = jnp.transpose(trailing_blocks[..., : seg_len - 1], (1, 0, 2))
    return lax.conv_general_dilated(
        source,
        kernel,
        (1,),
        "VALID",
        dimension_numbers=("NCH", "OIH", "CNH"),
        preferred_element_type=jnp.float32,
    )


def body(raw_traces, tile_pairs, block_slot, win_offset):
    owner_index = lax.axis_index("pairs")
    pair_count = lax.axis_size("pairs")
    win_count = lax.axis_size("win")
    local_channels = raw_traces.shape[2]
    channels = local_channels * pair_count
    seg_len = raw_traces.shape[3] - LAGS
    samples = seg_len - LAGS
    tile_count = tile_pairs.shape[1]
    segment = lax.dynamic_slice_in_dim(raw_traces[0], win_offset[0], seg_len, 2).astype(jnp.float32)
    whitened = whiten(segment)
    wanted = tile_pairs.reshape(pair_count, 2 * tile_count)
    slot_index = block_slot[jnp.maximum(wanted, 0)]
    outgoing = jnp.take(whitened, slot_index.reshape(-1), axis=0).reshape(
        pair_count, 2 * tile_count, local_channels, seg_len
    )
    incoming = lax.all_to_all(outgoing, "pairs", split_axis=0, concat_axis=2, tiled=True)
    blocks = incoming[0].reshape(tile_count, 2, channels, seg_len)
    own_tiles = lax.dynamic_index_in_dim(tile_pairs, owner_index, 0, keepdims=False)
    tile_valid = (own_tiles[:, 0] >= 0).astype(jnp.float32)
    firsts = blocks[:, 0]
    seconds = blocks[:, 1]
    row_share = channels // win_count
    spread_rows = lax.all_to_all(firsts[:, None], "win", split_axis=2, concat_axis=1, tiled=True)
    initial = jnp.zeros((row_share, tile_count, channels, LAGS), jnp.float32)
    piece = lax.all_gather(seconds[:, None], "win", axis=1, tiled=True)
    summed = initial + jnp.stack(
        [correlate(spread_rows[tile], piece[tile]) for tile in range(tile_count)], 1
    )
    scale = 1.0 / math.sqrt(win_count * samples)
    return summed * scale * tile_valid[None, :, None, None]


def solution(mesh):
    return jax.shard_map(
        body,
        mesh=mesh,
        in_specs=(P("win", None, "pairs", None), P(), P(), P("win")),
        out_specs=P("win", "pairs", None, None),
        check_vma=False,
    )
```

profile of v0, /device:TPU:1, one launch (start us, length us, event | category | flops | bytes accessed | tf_op | source)
XLA Modules:
  0.0 132.8 jit_solution(15492690190346590132)
XLA Ops:
  7.3 0.7 broadcast_maximum_fusion
  8.3 3.5 %gather_fusion = s32[512]{0:T(512)S(1)} fusion(s32[320]{0:T(512)S(1)} %copy-done.1, s32[1024]{0:T(1024)S(1)} %pad_clamp_fusion.1), kind=kCustom, calls=%fused_computation | custom fusion | bytes 6144 | tf_op jit(solution)/shard_map/gather | solution.py:60
  11.9 0.9 constant_dynamic-slice_fusion.1
  12.9 0.4 copy.88
  13.3 0.4 copy.89
  13.8 1.8 %fusion = f32[320,2,3,128]{0,3,2,1:T(8,128)S(1)} fusion(f32[320,2,3,128]{3,0,2,1:T(8,128)S(1)} %get-tuple-element.10, f32[320,2,3,128]{3,0,2,1:T(8,128)S(1)} %copy.89, f32[320,2,3,128]{3,0,2,1:T(8,128)S(1)} %get-tuple-element.9, s32[384]{0:T(512)S(1)} %iota_add_fusion), kind=kOutput, calls=%fused_computation.3 | convolution fusion | flops 1134084096 | bytes 3933696 | tf_op jit(solution)/shard_map/...ni,ij->...nj/dot_general | solution.py:22
  15.7 0.3 copy.92
  16.0 0.2 fusion.7
  16.2 0.5 copy.93
  16.7 3.1 %gather_fusion.1 = bf16[512,2,384]{2,1,0:T(2,128)(2,1)S(1)} fusion(bf16[320,2,384]{2,1,0:T(2,128)(2,1)S(1)} %copy.93, s32[1024]{0:T(1024)S(1)} %pad_clamp_fusion), kind=kCustom, calls=%fused_computation.1 | custom fusion | bytes 1574912 | tf_op jit(solution)/shard_map/jit(_take)/gather | solution.py:61
  19.8 0.2 bitcast_select_fusion
  20.1 35.5 %all_to_all.24 = bf16[64,8,2,384]{3,1,2,0:T(8,128)(2,1)S(1)} all-to-all(bf16[64,8,2,384]{3,1,2,0:T(8,128)(2,1)S(1)} %copy.95), channel_id=1, replica_groups=mesh['pairs'=64,'win'=4] {'pairs'}, dimensions={0} | all-to-all | bytes 1572864 | tf_op jit(solution)/shard_map/all_to_all | solution.py:64
  55.7 0.3 reshape.126
  56.0 1.1 fusion.24
  57.1 0.8 copy.136
  57.9 0.9 copy.99
  58.9 4.2 %all-to-all-start.1 = ((bf16[4,1,128,384]{3,0,1,2:T(4,128)(2,1)}), bf16[4,1,128,384]{3,0,1,2:T(4,128)(2,1)S(1)}, u32[]{:S(2)}, u32[]{:S(2)}) async-start(bf16[4,1,128,384]{3,0,1,2:T(4,128)(2,1)} %copy.99), calls=%async_computation.1 | async-start | bytes 786432 | tf_op jit(solution)/shard_map/all_to_all | solution.py:71
  63.2 6.4 %all-to-all-done.1 = bf16[4,1,128,384]{3,0,1,2:T(4,128)(2,1)S(1)} async-done(((bf16[4,1,128,384]{3,0,1,2:T(4,128)(2,1)}), bf16[4,1,128,384]{3,0,1,2:T(4,128)(2,1)S(1)}, u32[]{:S(2)}, u32[]{:S(2)}) %all-to-all-start.1) | async-done | bytes 393248 | tf_op jit(solution)/shard_map/all_to_all | solution.py:71
  69.6 0.6 fusion.25
  71.2 0.9 copy.121
  72.1 12.6 %all-gather.2.cloned.1.call-done = bf16[4,4,128,384]{3,2,0,1:T(8,128)(2,1)} async-done(((bf16[4,1,128,384]{3,2,0,1:T(8,128)(2,1)}), bf16[4,4,128,384]{3,2,0,1:T(8,128)(2,1)}) %all-gather.2.cloned.1.call-update) | async-done | bytes 1572880 | tf_op jit(solution)/shard_map/all_gather | solution.py:73
  84.6 1.5 %fusion.23 = (bf16[1,4,128,384]{3,2,0,1:T(8,128)(2,1)S(1)}, bf16[1,4,128,384]{3,2,0,1:T(8,128)(2,1)S(1)}, bf16[1,4,128,384]{3,2,0,1:T(8,128)(2,1)S(1)}, bf16[1,4,128,384]{3,2,0,1:T(8,128)(2,1)S(1)}) fusion(bf16[4,4,128,384]{3,2,0,1:T(8,128)(2,1)} %all-gather.2.cloned.1.call-done), kind=kLoop, calls=%fused_computation.48 | loop fusion | bytes 3145728 | tf_op jit(solution)/shard_map/slice | solution.py:75
  86.2 0.2 copy.118
  86.4 0.2 copy.125
  86.7 0.2 copy.122
  87.0 0.2 copy.128
  87.2 6.9 %convolution_bitcast_fusion.3 = f32[32,1,128,128]{2,0,3,1:T(8,128)S(1)} fusion(bf16[4,32,256]{1,0,2:T(4,128)(2,1)} %copy.121, bf16[1,4,128,384]{2,1,3,0:T(4,128)(2,1)S(1)} %copy.118), kind=kOutput, calls=%fused_computation.14 | convolution fusion | flops 1073741824 | bytes 2555904 | tf_op jit(solution)/shard_map/conv_general_dilated | solution.py:38
  94.1 5.9 %convolution_bitcast_fusion.1 = f32[32,1,128,128]{2,0,3,1:T(8,128)S(1)} fusion(bf16[4,32,256]{1,0,2:T(4,128)(2,1)S(1)} %copy.127, bf16[1,4,128,384]{2,1,3,0:T(4,128)(2,1)S(1)} %copy.125), kind=kOutput, calls=%fused_computation.12 | convolution fusion | flops 1073741824 | bytes 2555904 | tf_op jit(solution)/shard_map/conv_general_dilated | solution.py:38
  99.9 6.1 %convolution_bitcast_fusion.2 = f32[32,1,128,128]{2,0,3,1:T(8,128)S(1)} fusion(bf16[4,32,256]{1,0,2:T(4,128)(2,1)S(1)} %copy.124, bf16[1,4,128,384]{2,1,3,0:T(4,128)(2,1)S(1)} %copy.122), kind=kOutput, calls=%fused_computation.13 | convolution fusion | flops 1073741824 | bytes 2555904 | tf_op jit(solution)/shard_map/conv_general_dilated | solution.py:38
  106.0 5.9 %convolution_bitcast_fusion = f32[32,1,128,128]{2,0,3,1:T(8,128)S(1)} fusion(bf16[4,32,256]{1,0,2:T(4,128)(2,1)S(1)} %copy.130, bf16[1,4,128,384]{2,1,3,0:T(4,128)(2,1)S(1)} %copy.128), kind=kOutput, calls=%fused_computation.11 | convolution fusion | flops 1073741824 | bytes 2555904 | tf_op jit(solution)/shard_map/conv_general_dilated | solution.py:38
  111.9 4.1 %maximum_multiply_fusion = f32[32,4,128,128]{2,0,3,1:T(8,128)} fusion(f32[32,1,128,128]{2,0,3,1:T(8,128)S(1)} %convolution_bitcast_fusion, f32[32,1,128,128]{2,0,3,1:T(8,128)S(1)} %convolution_bitcast_fusion.1, f32[32,1,128,128]{2,0,3,1:T(8,128)S(1)} %convolution_bitcast_fusion.2, f32[32,1,128,128]{2,0,3,1:T(8,128)S(1)} %convolution_bitcast_fusion.3, ...), kind=kLoop, calls=%fused_computation.2 | loop fusion | flops 8388608 | bytes 16777232 | tf_op jit(solution)/shard_map/mul | solution.py:78
  116.0 9.9 %copy.112 = f32[32,4,128,128]{3,2,1,0:T(8,128)} copy(f32[32,4,128,128]{2,0,3,1:T(8,128)} %maximum_multiply_fusion) | data formatting | bytes 16777216 | tf_op jit(solution)/shard_map/mul | solution.py:78
  (34 shorter events, 1.9 us)
Async XLA Ops:
  6.5 5.4 %copy-start = (bf16[1,320,2,512]{3,2,1,0:T(2,128)(2,1)S(1)}, bf16[1,320,2,512]{3,2,1,0:T(2,128)(2,1)}, u32[]{:S(2)}) copy-start(bf16[1,320,2,512]{3,2,1,0:T(2,128)(2,1)} %param.4) | copy-start | bytes 1966084
  6.5 1.7 %copy-start.1 = (s32[320]{0:T(512)S(1)}, s32[320]{0:T(512)}, u32[]{:S(2)}) copy-start(s32[320]{0:T(512)} %param.6) | copy-start | bytes 3844
  6.5 78.1 %all-gather.2.cloned.1.call-start = ((), (), s32[]{:S(2)}) async-start(), calls=%async_computation.2 | async-start | bytes 1966080 | tf_op jit(solution)/shard_map/all_gather | solution.py:73
  57.1 6.0 %copy-start.2 = (s32[64,4,2]{0,2,1:T(2,128)S(1)}, s32[64,4,2]{0,2,1:T(2,128)}, u32[]{:S(2)}) copy-start(s32[64,4,2]{0,2,1:T(2,128)} %param.5) | copy-start | bytes 6148
  58.9 10.7 %all-to-all-start.1 = ((bf16[4,1,128,384]{3,0,1,2:T(4,128)(2,1)}), bf16[4,1,128,384]{3,0,1,2:T(4,128)(2,1)S(1)}, u32[]{:S(2)}, u32[]{:S(2)}) async-start(bf16[4,1,128,384]{3,0,1,2:T(4,128)(2,1)} %copy.99), calls=%async_computation.1 | async-start | bytes 786432 | tf_op jit(solution)/shard_map/all_to_all | solution.py:71
Sparse Core Ops, SparseCore 0:
  58.0 26.5 all-gather.1
where the time goes:
time: 133 us
  blocking collectives  35.5 us (27%)
  local copies, waits for them, and re-layouts  27.8 us (21%)
  matrix products  26.5 us (20%)
  waiting for transfers between devices  19 us (14%)
  between operations  14.4 us (11%)
  other arithmetic  5.36 us (4%)
  starting transfers between devices  4.18 us (3%)
    all_to_all x1, blocking collectives, body(): lax.all_to_all(outgoing, 'pairs', split_axis=0, concat_axis=2, tiled=True)  35.5 us
    conv_general_dilated x4, matrix products, correlate(): lax.conv_general_dilated(source, kernel, (1,), 'VALID', dimension_numbers...  24.7 us
    all_gather x1, waiting for transfers between devices, body(): piece = lax.all_gather(seconds[:, None], 'win', axis=1, tiled=True)  12.6 us
    mul x1, local copies, waits for them, and re-layouts, body(): return summed * scale * tile_valid[None, :, None, None]  9.9 us
    all_to_all x1, waiting for transfers between devices, body(): lax.all_to_all(firsts[:, None], 'win', split_axis=2, concat_axis=1, tiled...  6.37 us
    all_to_all x1, starting transfers between devices, body(): lax.all_to_all(firsts[:, None], 'win', split_axis=2, concat_axis=1, tiled...  4.18 us
    mul x2, other arithmetic, body(): return summed * scale * tile_valid[None, :, None, None]  4.14 us
    gather x2, local copies, waits for them, and re-layouts, body(): slot_index = block_slot[jnp.maximum(wanted, 0)]  3.57 us
  transfers between devices with their start and end apart: 2, of which 2 were waited for; matrix products, arithmetic and copies ran while one was open for 3% of the time, Pallas kernels for 0%

commit v1 on v0

--- a/solution.py
+++ b/solution.py
@@ -70,7 +70,11 @@
     row_share = channels // win_count
     spread_rows = lax.all_to_all(firsts[:, None], "win", split_axis=2, concat_axis=1, tiled=True)
     initial = jnp.zeros((row_share, tile_count, channels, LAGS), jnp.float32)
-    piece = lax.all_gather(seconds[:, None], "win", axis=1, tiled=True)
+    part = seconds[:, None]
+    size = lax.axis_size("win")
+    parts = jnp.stack([part for _ in range(size)])
+    parts = lax.all_to_all(parts, "win", split_axis=0, concat_axis=0)
+    piece = jnp.concatenate(parts, axis=1)
     summed = initial + jnp.stack(
         [correlate(spread_rows[tile], piece[tile]) for tile in range(tile_count)], 1
     )

time: 133 us -> 128 us (0.962)
  the two profiles are of different devices: /device:TPU:1 before, /device:TPU:32 now
where the time goes in v1:
time: 128 us; the launch traced here: 127 us
  blocking collectives  33.7 us (26%)
  local copies, waits for them, and re-layouts  27.5 us (21%)
  matrix products  25.8 us (20%)
  waiting for transfers between devices  25.6 us (20%)
  starting transfers between devices  8.21 us (6%)
  other arithmetic  5.36 us (4%)
    all_to_all x1, blocking collectives, body(): lax.all_to_all(outgoing, 'pairs', split_axis=0, concat_axis=2, tiled=True)  33.7 us
    conv_general_dilated x4, matrix products, correlate(): lax.conv_general_dilated(source, kernel, (1,), 'VALID', dimension_numbers...  23.9 us
    all_to_all x1, waiting for transfers between devices, body(): parts = lax.all_to_all(parts, 'win', split_axis=0, concat_axis=0)  18.1 us
    mul x1, local copies, waits for them, and re-layouts, body(): return summed * scale * tile_valid[None, :, None, None]  9.9 us
    all_to_all x1, waiting for transfers between devices, body(): lax.all_to_all(firsts[:, None], 'win', split_axis=2, concat_axis=1, tiled...  7.5 us
    all_to_all x1, starting transfers between devices, body(): lax.all_to_all(firsts[:, None], 'win', split_axis=2, concat_axis=1, tiled...  4.46 us
    mul x2, other arithmetic, body(): return summed * scale * tile_valid[None, :, None, None]  4.13 us
    all_to_all x1, starting transfers between devices, body(): parts = lax.all_to_all(parts, 'win', split_axis=0, concat_axis=0)  3.74 us
  transfers between devices with their start and end apart: 2, of which 2 were waited for; matrix products, arithmetic and copies ran while one was open for 2% of the time, Pallas kernels for 0%

profile of v1, /device:TPU:32, one launch (start us, length us, event | category | flops | bytes accessed | tf_op | source)
XLA Modules:
  0.0 127.2 jit_solution(10189922814773484724)
XLA Ops:
  0.7 0.7 broadcast_maximum_fusion
  1.8 3.5 %gather_fusion = s32[512]{0:T(512)S(1)} fusion(s32[320]{0:T(512)S(1)} %copy-done.1, s32[1024]{0:T(1024)S(1)} %pad_clamp_fusion.1), kind=kCustom, calls=%fused_computation | custom fusion | bytes 6144 | tf_op jit(solution)/shard_map/gather | solution.py:60
  5.4 0.9 constant_dynamic-slice_fusion.1
  6.4 0.4 copy.83
  6.8 0.4 copy.84
  7.3 1.8 %fusion = f32[320,2,3,128]{0,3,2,1:T(8,128)S(1)} fusion(f32[320,2,3,128]{3,0,2,1:T(8,128)S(1)} %get-tuple-element.6, f32[320,2,3,128]{3,0,2,1:T(8,128)S(1)} %copy.84, f32[320,2,3,128]{3,0,2,1:T(8,128)S(1)} %get-tuple-element.5, s32[384]{0:T(512)S(1)} %iota_add_fusion), kind=kOutput, calls=%fused_computation.3 | convolution fusion | flops 1134084096 | bytes 3933696 | tf_op jit(solution)/shard_map/...ni,ij->...nj/dot_general | solution.py:22
  9.1 0.3 copy.87
  9.5 0.2 fusion.7
  9.7 0.5 copy.88
  10.2 3.1 %gather_fusion.1 = bf16[512,2,384]{2,1,0:T(2,128)(2,1)S(1)} fusion(bf16[320,2,384]{2,1,0:T(2,128)(2,1)S(1)} %copy.88, s32[1024]{0:T(1024)S(1)} %pad_clamp_fusion), kind=kCustom, calls=%fused_computation.1 | custom fusion | bytes 1574912 | tf_op jit(solution)/shard_map/jit(_take)/gather | solution.py:61
  13.3 0.2 bitcast_select_fusion
  13.6 33.7 %all_to_all.29 = bf16[64,8,2,384]{3,1,2,0:T(8,128)(2,1)S(1)} all-to-all(bf16[64,8,2,384]{3,1,2,0:T(8,128)(2,1)S(1)} %copy.90), channel_id=1, replica_groups=mesh['pairs'=64,'win'=4] {'pairs'}, dimensions={0} | all-to-all | bytes 1572864 | tf_op jit(solution)/shard_map/all_to_all | solution.py:64
  47.3 0.3 reshape.142
  47.6 1.1 fusion.19
  48.7 0.9 copy.94
  49.6 4.5 %all-to-all-start.2 = ((bf16[4,1,128,384]{3,0,1,2:T(4,128)(2,1)}), bf16[4,1,128,384]{3,0,1,2:T(4,128)(2,1)S(1)}, u32[]{:S(2)}, u32[]{:S(2)}) async-start(bf16[4,1,128,384]{3,0,1,2:T(4,128)(2,1)} %copy.94), calls=%async_computation.2 | async-start | bytes 786432 | tf_op jit(solution)/shard_map/all_to_all | solution.py:71
  54.1 1.0 copy.120
  55.2 7.5 %all-to-all-done.2 = bf16[4,1,128,384]{3,0,1,2:T(4,128)(2,1)S(1)} async-done(((bf16[4,1,128,384]{3,0,1,2:T(4,128)(2,1)}), bf16[4,1,128,384]{3,0,1,2:T(4,128)(2,1)S(1)}, u32[]{:S(2)}, u32[]{:S(2)}) %all-to-all-start.2) | async-done | bytes 393248 | tf_op jit(solution)/shard_map/all_to_all | solution.py:71
  62.7 1.4 %stack.18 = bf16[4,4,1,128,384]{3,4,2,1,0:T(8,128)(2,1)} broadcast(bf16[4,128,384]{1,2,0:T(8,128)(2,1)S(1)} %bitcast.70), dimensions={1,3,4} | broadcast | bytes 1966080 | tf_op jit(solution)/shard_map/stack | solution.py:75
  64.1 3.7 %all-to-all-start.1 = ((bf16[4,4,1,128,384]{3,4,2,1,0:T(8,128)(2,1)}), bf16[4,4,1,128,384]{3,4,2,1,0:T(8,128)(2,1)S(1)}, u32[]{:S(2)}, u32[]{:S(2)}) async-start(bf16[4,4,1,128,384]{3,4,2,1,0:T(8,128)(2,1)} %stack.18), calls=%async_computation.1 | async-start | bytes 3145728 | tf_op jit(solution)/shard_map/all_to_all | solution.py:76
  68.1 0.6 fusion.20
  69.3 0.2 copy.114
  69.5 0.2 copy.116
  69.7 0.2 copy.112
  69.9 18.1 %all-to-all-done.1 = bf16[4,4,1,128,384]{3,4,2,1,0:T(8,128)(2,1)S(1)} async-done(((bf16[4,4,1,128,384]{3,4,2,1,0:T(8,128)(2,1)}), bf16[4,4,1,128,384]{3,4,2,1,0:T(8,128)(2,1)S(1)}, u32[]{:S(2)}, u32[]{:S(2)}) %all-to-all-start.1) | async-done | bytes 1572896 | tf_op jit(solution)/shard_map/all_to_all | solution.py:76
  88.0 1.2 copy.125
  89.2 5.9 %convolution_bitcast_fusion = f32[32,1,128,128]{2,0,3,1:T(8,128)S(1)} fusion(bf16[4,32,256]{1,0,2:T(4,128)(2,1)S(1)} %copy.118, bf16[4,4,1,128,384]{3,1,4,2,0:T(4,128)(2,1)S(1)} %bitcast.66), kind=kOutput, calls=%fused_computation.11 | convolution fusion | flops 1073741824 | bytes 2752512 | tf_op jit(solution)/shard_map/conv_general_dilated | solution.py:38
  95.2 5.9 %convolution_bitcast_fusion.1 = f32[32,1,128,128]{2,0,3,1:T(8,128)S(1)} fusion(bf16[4,32,256]{1,0,2:T(4,128)(2,1)S(1)} %copy.116, bf16[4,4,1,128,384]{3,1,4,2,0:T(4,128)(2,1)S(1)} %bitcast.67), kind=kOutput, calls=%fused_computation.12 | convolution fusion | flops 1073741824 | bytes 2752512 | tf_op jit(solution)/shard_map/conv_general_dilated | solution.py:38
  101.1 6.1 %convolution_bitcast_fusion.2 = f32[32,1,128,128]{2,0,3,1:T(8,128)S(1)} fusion(bf16[4,32,256]{1,0,2:T(4,128)(2,1)S(1)} %copy.114, bf16[4,4,1,128,384]{3,1,4,2,0:T(4,128)(2,1)S(1)} %bitcast.68), kind=kOutput, calls=%fused_computation.13 | convolution fusion | flops 1073741824 | bytes 2752512 | tf_op jit(solution)/shard_map/conv_general_dilated | solution.py:38
  107.2 5.9 %convolution_bitcast_fusion.3 = f32[32,1,128,128]{2,0,3,1:T(8,128)S(1)} fusion(bf16[4,32,256]{1,0,2:T(4,128)(2,1)S(1)} %copy.112, bf16[4,4,1,128,384]{3,1,4,2,0:T(4,128)(2,1)S(1)} %bitcast.69), kind=kOutput, calls=%fused_computation.14 | convolution fusion | flops 1073741824 | bytes 2752512 | tf_op jit(solution)/shard_map/conv_general_dilated | solution.py:38
  113.1 4.1 %maximum_multiply_fusion = f32[32,4,128,128]{2,0,3,1:T(8,128)} fusion(f32[32,1,128,128]{2,0,3,1:T(8,128)S(1)} %convolution_bitcast_fusion, f32[32,1,128,128]{2,0,3,1:T(8,128)S(1)} %convolution_bitcast_fusion.1, f32[32,1,128,128]{2,0,3,1:T(8,128)S(1)} %convolution_bitcast_fusion.2, f32[32,1,128,128]{2,0,3,1:T(8,128)S(1)} %convolution_bitcast_fusion.3, ...), kind=kLoop, calls=%fused_computation.2 | loop fusion | flops 8388608 | bytes 16777232 | tf_op jit(solution)/shard_map/mul | solution.py:82
  117.3 9.9 %copy.104 = f32[32,4,128,128]{3,2,1,0:T(8,128)} copy(f32[32,4,128,128]{2,0,3,1:T(8,128)} %maximum_multiply_fusion) | data formatting | bytes 16777216 | tf_op jit(solution)/shard_map/mul | solution.py:82
  (30 shorter events, 1.5 us)
Async XLA Ops:
  0.0 5.4 %copy-start = (bf16[1,320,2,512]{3,2,1,0:T(2,128)(2,1)S(1)}, bf16[1,320,2,512]{3,2,1,0:T(2,128)(2,1)}, u32[]{:S(2)}) copy-start(bf16[1,320,2,512]{3,2,1,0:T(2,128)(2,1)} %param.4) | copy-start | bytes 1966084
  0.0 1.7 %copy-start.1 = (s32[320]{0:T(512)S(1)}, s32[320]{0:T(512)}, u32[]{:S(2)}) copy-start(s32[320]{0:T(512)} %param.6) | copy-start | bytes 3844
  49.6 13.0 %all-to-all-start.2 = ((bf16[4,1,128,384]{3,0,1,2:T(4,128)(2,1)}), bf16[4,1,128,384]{3,0,1,2:T(4,128)(2,1)S(1)}, u32[]{:S(2)}, u32[]{:S(2)}) async-start(bf16[4,1,128,384]{3,0,1,2:T(4,128)(2,1)} %copy.94), calls=%async_computation.2 | async-start | bytes 786432 | tf_op jit(solution)/shard_map/all_to_all | solution.py:71
  62.7 5.2 %copy-start.2 = (s32[64,4,2]{0,2,1:T(2,128)S(1)}, s32[64,4,2]{0,2,1:T(2,128)}, u32[]{:S(2)}) copy-start(s32[64,4,2]{0,2,1:T(2,128)} %param.5) | copy-start | bytes 6148
  64.1 23.9 %all-to-all-start.1 = ((bf16[4,4,1,128,384]{3,4,2,1,0:T(8,128)(2,1)}), bf16[4,4,1,128,384]{3,4,2,1,0:T(8,128)(2,1)S(1)}, u32[]{:S(2)}, u32[]{:S(2)}) async-start(bf16[4,4,1,128,384]{3,4,2,1,0:T(8,128)(2,1)} %stack.18), calls=%async_computation.1 | async-start | bytes 3145728 | tf_op jit(solution)/shard_map/all_to_all | solution.py:76
